TPU v7x, 128 devices: a whole 4x4x4 slice. The times are simulated.
128 devices in a mesh: row: 8 (over z, y_lo), col: 16 (over y_hi, x, core).
Axes of the slice: x: 4, y: 4 (y_hi: 2, y_lo: 2; y = y_hi * 2 + y_lo), z: 4, core: 2. Of those that a mesh axis runs over, the one named last changes fastest.
Arguments:
- blocks: float32 [8, 16, 170, 128, 128], P('row', 'col'), may hold values from -1 to 1
- coords: int32 [8, 16, 2, 170], P('row', 'col'), may hold values from 0 to 31, as said below
- vectors: float32 [2, 32768, 128], P(None, ('row', 'col')), may hold values from -6 to 6
Outputs:
- basis: float32 [2, 32768, 128], P(None, ('row', 'col'))
Inputs may be any that keep to these rules, and one draw needn't show every extreme that they name: Within each tile the 170 listed positions are distinct, and the positions (0, 0) and (31, 15) are always listed; coords[r, c, 0, k] is below 32 and coords[r, c, 1, k] below 16.
All inputs are finite; a program needn't handle non-finite values.
Results may differ from a plain program's by a relative error of at most 0.0003.
Values sent between devices are 32-bit elements; how exact they have to be, the bound alone decides.
A program may use at most 192 MiB of HBM per device.

v0:
```python
import jax
import jax.numpy as jnp
from jax import lax
from jax.sharding import PartitionSpec as P

APPS = 2
exact_mode = lax.Precision.HIGHEST


def tile_products(values, places, col_side, row_side):
    blk_size = values.shape[1]
    listed = values.shape[0]
    row_blocks = row_side.shape[0] // blk_size
    col_blocks = col_side.shape[0] // blk_size
    row_of = places[0]
    col_of = places[1]
    col_pieces = col_side.reshape(col_blocks, blk_size, -1)[col_of]
    direct = jnp.einsum("kab,kbv->kav", values, col_pieces, precision=exact_mode)
    row_pieces = row_side.reshape(row_blocks, blk_size, -1)[row_of]
    flipped = jnp.einsum("kba,kbv->kav", values, row_pieces, precision=exact_mode)
    row_hot = (row_of[None, :] == jnp.arange(row_blocks, dtype=jnp.int32)[:, None]).astype(
        values.dtype
    )
    col_hot = (col_of[None, :] == jnp.arange(col_blocks, dtype=jnp.int32)[:, None]).astype(
        values.dtype
    )
    out_rows = jnp.dot(row_hot, direct.reshape(listed, -1), precision=exact_mode).reshape(
        row_side.shape[0], -1
    )
    out_cols = jnp.dot(col_hot, flipped.reshape(listed, -1), precision=exact_mode).reshape(
        col_side.shape[0], -1
    )
    return (out_rows, out_cols)


def normal_basis(applied, factor):
    return lax.linalg.triangular_solve(
        factor, applied, left_side=False, lower=True, transpose_a=True
    )


def local(blocks, coords, vectors):
    n_rowdev = lax.axis_size("row")
    n_coldev = lax.axis_size("col")
    group_rows = vectors.shape[1]
    total_rows = 2 * group_rows * n_rowdev * n_coldev
    values = blocks.reshape(blocks.shape[2], blocks.shape[3], blocks.shape[4])
    places = coords.reshape(2, coords.shape[3])
    start = (vectors[0], vectors[1])
    current = start
    for app_index in range(APPS):
        col_side = lax.all_gather(current[1], "row", axis=0, tiled=True)
        row_side = lax.all_gather(current[0], "col", axis=0, tiled=True)
        out_rows, out_cols = tile_products(values, places, col_side, row_side)
        new_upper = lax.psum_scatter(out_rows, "col", scatter_dimension=0, tiled=True)
        new_lower = lax.psum_scatter(out_cols, "row", scatter_dimension=0, tiled=True)
        applied = (new_upper, new_lower)
        factor_upper, factor_lower = applied
        partial_gram = jnp.einsum("nv,nw->vw", factor_upper, factor_upper, precision=exact_mode)
        partial_gram = partial_gram + jnp.einsum(
            "nv,nw->vw", factor_lower, factor_lower, precision=exact_mode
        )
        gram_sum = lax.psum(partial_gram, ("row", "col")) / total_rows
        factor = jnp.linalg.cholesky(gram_sum)
        current = (normal_basis(applied[0], factor), normal_basis(applied[1], factor))
    upper, lower = current
    return jnp.stack([upper, lower])


def solution(mesh):
    return jax.shard_map(
        local,
        mesh=mesh,
        in_specs=(
            P("row", "col", None, None, None),
            P("row", "col", None, None),
            P(None, ("row", "col"), None),
        ),
        out_specs=P(None, ("row", "col"), None),
        check_vma=False,
    )
```

profile of v0, /device:TPU:1, one launch (start us, length us, event | category | flops | bytes accessed | tf_op | source)
XLA Modules:
  0.0 845.6 jit_solution(6474394078749091209)
XLA Ops:
  10.6 37.6 %all-gather.11.cloned.1.call-done = f32[1,2048,128]{2,1,0:T(8,128)} async-done(((f32[1,256,128]{2,1,0:T(8,128)}), f32[1,2048,128]{2,1,0:T(8,128)}) %all-gather.11.cloned.1.call-update) | async-done | bytes 1048592 | tf_op jit(solution)/shard_map/all_gather | solution.py:52
  48.2 11.6 %gather_fusion = f32[170,128,128]{2,1,0:T(8,128)} fusion(f32[16,128,128]{2,1,0:T(8,128)} %bitcast.108, s32[1024]{0:T(1024)S(1)} %pad_clamp_fusion.1), kind=kCustom, calls=%fused_computation | custom fusion | bytes 22282920 | tf_op jit(solution)/shard_map/gather | solution.py:17
  59.8 23.3 %fusion.8 = f32[170,128,128]{1,2,0:T(8,128)} fusion(f32[170,128,128]{2,1,0:T(8,128)} %gather_fusion, f32[1,1,170,128,128]{4,3,2,1,0:T(8,128)} %param.6), kind=kOutput, calls=%fused_computation.12 | convolution fusion | flops 4278190080 | bytes 33423360 | tf_op jit(solution)/shard_map/kab,kbv->kav/dot_general | solution.py:18
  83.1 12.3 %copy.12 = f32[170,128,128]{2,1,0:T(8,128)} copy(f32[170,128,128]{1,2,0:T(8,128)} %fusion.8) | data formatting | bytes 22282240 | tf_op jit(solution)/shard_map/kab,kbv->kav/dot_general | solution.py:18
  95.3 10.5 %pad.6 = f32[176,128,128]{2,1,0:T(8,128)} pad(f32[170,128,128]{2,1,0:T(8,128)} %copy.12, f32[]{:T(128)} %constant.31.clone.2), padding=0_6x0_0x0_0 | pad | bytes 22675460
  105.8 18.3 %copy.38 = f32[22,8,128,128]{3,1,2,0:T(8,128)} copy(f32[22,8,128,128]{3,2,1,0:T(8,128)} %bitcast.115) | data formatting | bytes 23068672
  132.8 12.0 %gather_fusion.1 = f32[170,128,128]{2,1,0:T(8,128)} fusion(f32[32,128,128]{2,1,0:T(8,128)} %bitcast.110, s32[1024]{0:T(1024)S(1)} %pad_clamp_fusion), kind=kCustom, calls=%fused_computation.1 | custom fusion | bytes 22282920 | tf_op jit(solution)/shard_map/gather | solution.py:19
  144.8 23.4 %fusion.11 = f32[170,128,128]{1,2,0:T(8,128)} fusion(f32[170,128,128]{2,1,0:T(8,128)} %gather_fusion.1, f32[1,1,170,128,128]{4,3,2,1,0:T(8,128)} %param.6), kind=kOutput, calls=%fused_computation.13 | convolution fusion | flops 4278190080 | bytes 33423360 | tf_op jit(solution)/shard_map/kba,kbv->kav/dot_general | solution.py:20
  168.2 12.0 %copy.14 = f32[170,128,128]{2,1,0:T(8,128)} copy(f32[170,128,128]{1,2,0:T(8,128)} %fusion.11) | data formatting | bytes 22282240 | tf_op jit(solution)/shard_map/kba,kbv->kav/dot_general | solution.py:20
  180.3 10.4 %pad.7 = f32[176,128,128]{2,1,0:T(8,128)} pad(f32[170,128,128]{2,1,0:T(8,128)} %copy.14, f32[]{:T(128)} %constant.31.clone.2), padding=0_6x0_0x0_0 | pad | bytes 22675460
  190.7 18.4 %copy.39 = f32[22,8,128,128]{3,1,2,0:T(8,128)} copy(f32[22,8,128,128]{3,2,1,0:T(8,128)} %bitcast.117) | data formatting | bytes 23068672
  218.7 39.3 %reduce-scatter.7.cloned.1.call-done = f32[256,128]{1,0:T(8,128)} async-done(((f32[2048,128]{1,0:T(8,128)}), f32[256,128]{1,0:T(8,128)}) %reduce-scatter.7.cloned.1.call-update) | async-done | bytes 131088 | tf_op jit(solution)/shard_map/reduce_scatter | solution.py:56
  260.0 144.0 %all-reduce.3.cloned.1.call-done = f32[128,128]{0,1:T(8,128)} async-done(((f32[128,128]{0,1:T(8,128)}), f32[128,128]{0,1:T(8,128)}) %all-reduce.3.cloned.1.call-update) | async-done | bytes 65552 | tf_op jit(solution)/shard_map/psum | solution.py:63
  405.8 11.7 %cholesky.44 = f32[128,128]{1,0:T(8,128)S(1)} custom-call(f32[128,128]{1,0:T(8,128)S(1)} %fusion.27), custom_call_target="Cholesky" | custom-call | tf_op jit(solution)/shard_map/jit(cholesky)/cholesky | solution.py:64
  432.6 31.0 %all-gather.7.cloned.1.call-done = f32[2048,128]{0,1:T(8,128)} async-done(((f32[256,128]{0,1:T(8,128)}), f32[2048,128]{0,1:T(8,128)}) %all-gather.7.cloned.1.call-update) | async-done | bytes 1048592 | tf_op jit(solution)/shard_map/all_gather | solution.py:52
  470.5 23.5 %fusion.14 = f32[170,128,128]{1,2,0:T(8,128)} fusion(f32[170,128,128]{2,1,0:T(8,128)} %gather_fusion.2, f32[1,1,170,128,128]{4,3,2,1,0:T(8,128)} %param.6), kind=kOutput, calls=%fused_computation.14 | convolution fusion | flops 4278190080 | bytes 33423360 | tf_op jit(solution)/shard_map/kab,kbv->kav/dot_general | solution.py:18
  494.0 12.1 %copy.20 = f32[170,128,128]{2,1,0:T(8,128)} copy(f32[170,128,128]{1,2,0:T(8,128)} %fusion.14) | data formatting | bytes 22282240 | tf_op jit(solution)/shard_map/kab,kbv->kav/dot_general | solution.py:18
  516.4 18.4 %copy.40 = f32[22,8,128,128]{3,1,2,0:T(8,128)} copy(f32[22,8,128,128]{3,2,1,0:T(8,128)} %bitcast.118) | data formatting | bytes 23068672
  550.9 23.4 %fusion.17 = f32[170,128,128]{1,2,0:T(8,128)} fusion(f32[170,128,128]{2,1,0:T(8,128)} %gather_fusion.3, f32[1,1,170,128,128]{4,3,2,1,0:T(8,128)} %param.6), kind=kOutput, calls=%fused_computation.15 | convolution fusion | flops 4278190080 | bytes 33423360 | tf_op jit(solution)/shard_map/kba,kbv->kav/dot_general | solution.py:20
  574.3 12.0 %copy.23 = f32[170,128,128]{2,1,0:T(8,128)} copy(f32[170,128,128]{1,2,0:T(8,128)} %fusion.17) | data formatting | bytes 22282240 | tf_op jit(solution)/shard_map/kba,kbv->kav/dot_general | solution.py:20
  596.7 18.3 %copy.41 = f32[22,8,128,128]{3,1,2,0:T(8,128)} copy(f32[22,8,128,128]{3,2,1,0:T(8,128)} %bitcast.113) | data formatting | bytes 23068672
  624.4 39.4 %reduce-scatter.11.cloned.1.call-done = f32[256,128]{1,0:T(8,128)} async-done(((f32[2048,128]{1,0:T(8,128)}), f32[256,128]{1,0:T(8,128)}) %reduce-scatter.11.cloned.1.call-update) | async-done | bytes 131088 | tf_op jit(solution)/shard_map/reduce_scatter | solution.py:56
  665.8 144.7 %all-reduce.5.cloned.1.call-done = f32[128,128]{0,1:T(8,128)} async-done(((f32[128,128]{0,1:T(8,128)}), f32[128,128]{0,1:T(8,128)}) %all-reduce.5.cloned.1.call-update) | async-done | bytes 65552 | tf_op jit(solution)/shard_map/psum | solution.py:63
  812.4 11.7 %cholesky.55 = f32[128,128]{1,0:T(8,128)S(1)} custom-call(f32[128,128]{1,0:T(8,128)S(1)} %fusion.24), custom_call_target="Cholesky" | custom-call | tf_op jit(solution)/shard_map/jit(cholesky)/cholesky | solution.py:64
  (67 shorter events, 112.4 us)
Async XLA Ops:
  6.5 41.7 %all-gather.11.cloned.1.call-start = ((), (), s32[]{:S(2)}) async-start(), calls=%async_computation.12 | async-start | bytes 1179648 | tf_op jit(solution)/shard_map/all_gather | solution.py:52
  8.2 124.6 %all-gather.13.cloned.1.call-start = ((), (), s32[]{:S(2)}) async-start(), calls=%async_computation.13 | async-start | bytes 2228224 | tf_op jit(solution)/shard_map/all_gather | solution.py:53
  9.0 208.3 %reduce-scatter.5.cloned.1.call-start = ((), (), s32[]{:S(2)}) async-start(), calls=%async_computation.4 | async-start | bytes 2228224 | tf_op jit(solution)/shard_map/reduce_scatter | solution.py:55
  132.7 125.2 %reduce-scatter.7.cloned.1.call-start = ((), (), s32[]{:S(2)}) async-start(), calls=%async_computation.5 | async-start | bytes 1179648 | tf_op jit(solution)/shard_map/reduce_scatter | solution.py:56
  217.2 186.8 %all-reduce.3.cloned.1.call-start = ((), (), s32[]{:S(2)}) async-start(), calls=%async_computation.6 | async-start | bytes 131072 | tf_op jit(solution)/shard_map/psum | solution.py:63
  260.0 203.6 %all-gather.7.cloned.1.call-start = ((), (), s32[]{:S(2)}) async-start(), calls=%async_computation.7 | async-start | bytes 1179648 | tf_op jit(solution)/shard_map/all_gather | solution.py:52
  430.6 113.1 %all-gather.9.cloned.1.call-start = ((), (), s32[]{:S(2)}) async-start(), calls=%async_computation.9 | async-start | bytes 2228224 | tf_op jit(solution)/shard_map/all_gather | solution.py:53
  432.5 190.5 %reduce-scatter.9.cloned.1.call-start = ((), (), s32[]{:S(2)}) async-start(), calls=%async_computation.8 | async-start | bytes 2228224 | tf_op jit(solution)/shard_map/reduce_scatter | solution.py:55
  543.6 120.2 %reduce-scatter.11.cloned.1.call-start = ((), (), s32[]{:S(2)}) async-start(), calls=%async_computation.10 | async-start | bytes 1179648 | tf_op jit(solution)/shard_map/reduce_scatter | solution.py:56
  623.0 187.6 %all-reduce.5.cloned.1.call-start = ((), (), s32[]{:S(2)}) async-start(), calls=%async_computation.11 | async-start | bytes 131072 | tf_op jit(solution)/shard_map/psum | solution.py:63
Sparse Core Ops, SparseCore 0:
  9.0 39.1 all-gather.10
  50.6 52.7 all-gather.12
  132.9 73.0 reduce-scatter.4
  217.4 40.5 reduce-scatter.6
  262.5 141.4 all-reduce.2
  430.7 32.8 all-gather.6
  466.1 53.9 all-gather.8
  543.7 73.1 reduce-scatter.8
  623.1 40.6 reduce-scatter.10
  669.1 141.4 all-reduce.4
where the time goes:
time: 855 us; the launch traced here: 846 us
  waiting for transfers between devices  437 us (51%)
  local copies, waits for them, and re-layouts  210 us (25%)
  matrix products  135 us (16%)
  other arithmetic  49.9 us (6%)
  between operations  14 us (2%)
    psum x2, waiting for transfers between devices, local(): gram_sum = lax.psum(partial_gram, ('row', 'col')) / total_rows  289 us
    unnamed x8, local copies, waits for them, and re-layouts  115 us
    reduce_scatter x2, waiting for transfers between devices, local(): lax.psum_scatter(out_cols, 'row', scatter_dimension=0, tiled=True)  78.7 us
    all_gather x2, waiting for transfers between devices, local(): col_side = lax.all_gather(current[1], 'row', axis=0, tiled=True)  68.6 us
    dot_general x2, matrix products, tile_products(): jnp.einsum('kab,kbv->kav', values, col_pieces, precision=exact_mode)  46.9 us
    dot_general x2, matrix products, tile_products(): jnp.einsum('kba,kbv->kav', values, row_pieces, precision=exact_mode)  46.8 us
    another operation x6, other arithmetic, local(): factor = jnp.linalg.cholesky(gram_sum)  24.8 us
    dot_general x2, local copies, waits for them, and re-layouts, tile_products(): jnp.einsum('kab,kbv->kav', values, col_pieces, precision=exact_mode)  24.3 us
  transfers between devices with their start and end apart: 10, of which 6 were waited for; matrix products, arithmetic and copies ran while one was open for 40% of the time, Pallas kernels for 0%

commit v1 on v0

--- a/solution.py
+++ b/solution.py
@@ -49,7 +49,9 @@
     start = (vectors[0], vectors[1])
     current = start
     for app_index in range(APPS):
-        col_side = lax.all_gather(current[1], "row", axis=0, tiled=True)
+        col_side = jnp.concatenate(
+            lax.all_to_all(jnp.stack([current[1]] * lax.axis_size("row")), "row", 0, 0), axis=0
+        )
         row_side = lax.all_gather(current[0], "col", axis=0, tiled=True)
         out_rows, out_cols = tile_products(values, places, col_side, row_side)
         new_upper = lax.psum_scatter(out_rows, "col", scatter_dimension=0, tiled=True)

time: 855 us -> 807 us (0.944)
  waiting for transfers between devices: 437 us -> 370 us
  blocking collectives: 0 us -> 20.2 us
    all_gather x2 -> x0, waiting for transfers between devices: 68.6 us -> none  [local(): col_side = lax.all_gather(current[1], 'row', axis=0, tiled=True)]
    all_to_all x0 -> x1, blocking collectives: none -> 20.2 us  [local(): lax.all_to_all(jnp.stack([current[1]] * lax.axis_size('row')), 'row', 0, 0)]
    all_to_all x0 -> x1, waiting for transfers between devices: none -> 14.3 us  [local(): lax.all_to_all(jnp.stack([current[1]] * lax.axis_size('row')), 'row', 0, 0)]
    reduce_scatter x2, waiting for transfers between devices: 78.7 us -> 67.1 us  [local(): lax.psum_scatter(out_cols, 'row', scatter_dimension=0, tiled=True)]
  transfers between devices with their start and end apart: 10 -> 9, of which waited for: 6 -> 5; matrix products, arithmetic and copies ran while one was open for 40% -> 41% of each run, Pallas kernels for 0% -> 0%
where the time goes in v1:
time: 807 us; the launch traced here: 799 us
  waiting for transfers between devices  370 us (46%)
  local copies, waits for them, and re-layouts  203 us (25%)
  matrix products  134 us (17%)
  other arithmetic  49.9 us (6%)
  blocking collectives  20.2 us (3%)
  between operations  14 us (2%)
    psum x2, waiting for transfers between devices, local(): gram_sum = lax.psum(partial_gram, ('row', 'col')) / total_rows  289 us
    unnamed x8, local copies, waits for them, and re-layouts  115 us
    reduce_scatter x2, waiting for transfers between devices, local(): lax.psum_scatter(out_cols, 'row', scatter_dimension=0, tiled=True)  67.1 us
    dot_general x2, matrix products, tile_products(): jnp.einsum('kba,kbv->kav', values, row_pieces, precision=exact_mode)  47.1 us
    dot_general x2, matrix products, tile_products(): jnp.einsum('kab,kbv->kav', values, col_pieces, precision=exact_mode)  46.9 us
    another operation x6, other arithmetic, local(): factor = jnp.linalg.cholesky(gram_sum)  24.8 us
    dot_general x2, local copies, waits for them, and re-layouts, tile_products(): jnp.einsum('kab,kbv->kav', values, col_pieces, precision=exact_mode)  24.3 us
    dot_general x2, local copies, waits for them, and re-layouts, tile_products(): jnp.einsum('kba,kbv->kav', values, row_pieces, precision=exact_mode)  24.1 us
  transfers between devices with their start and end apart: 9, of which 5 were waited for; matrix products, arithmetic and copies ran while one was open for 41% of the time, Pallas kernels for 0%

profile of v1, /device:TPU:1, one launch (start us, length us, event | category | flops | bytes accessed | tf_op | source)
XLA Modules:
  0.0 799.3 jit_solution(5458482885631119530)
XLA Ops:
  17.7 14.3 %all-to-all-done = f32[8,256,128]{2,1,0:T(8,128)S(1)} async-done(((f32[8,256,128]{2,1,0:T(8,128)}), f32[8,256,128]{2,1,0:T(8,128)S(1)}, u32[]{:S(2)}, u32[]{:S(2)}) %all-to-all-start) | async-done | bytes 1048608 | tf_op jit(solution)/shard_map/all_to_all | solution.py:53
  37.4 23.4 %fusion.8 = f32[170,128,128]{1,2,0:T(8,128)} fusion(f32[170,128,128]{2,1,0:T(8,128)} %gather_fusion, f32[1,1,170,128,128]{4,3,2,1,0:T(8,128)} %param.6), kind=kOutput, calls=%fused_computation.12 | convolution fusion | flops 4278190080 | bytes 33423360 | tf_op jit(solution)/shard_map/kab,kbv->kav/dot_general | solution.py:18
  60.8 12.3 %copy.13 = f32[170,128,128]{2,1,0:T(8,128)} copy(f32[170,128,128]{1,2,0:T(8,128)} %fusion.8) | data formatting | bytes 22282240 | tf_op jit(solution)/shard_map/kab,kbv->kav/dot_general | solution.py:18
  83.4 18.3 %copy.38 = f32[22,8,128,128]{3,1,2,0:T(8,128)} copy(f32[22,8,128,128]{3,2,1,0:T(8,128)} %bitcast.117) | data formatting | bytes 23068672
  110.4 12.1 %gather_fusion.1 = f32[170,128,128]{2,1,0:T(8,128)} fusion(f32[32,128,128]{2,1,0:T(8,128)} %bitcast.112, s32[1024]{0:T(1024)S(1)} %pad_clamp_fusion), kind=kCustom, calls=%fused_computation.1 | custom fusion | bytes 22282920 | tf_op jit(solution)/shard_map/gather | solution.py:19
  122.5 23.5 %fusion.11 = f32[170,128,128]{1,2,0:T(8,128)} fusion(f32[170,128,128]{2,1,0:T(8,128)} %gather_fusion.1, f32[1,1,170,128,128]{4,3,2,1,0:T(8,128)} %param.6), kind=kOutput, calls=%fused_computation.13 | convolution fusion | flops 4278190080 | bytes 33423360 | tf_op jit(solution)/shard_map/kba,kbv->kav/dot_general | solution.py:20
  146.0 12.0 %copy.15 = f32[170,128,128]{2,1,0:T(8,128)} copy(f32[170,128,128]{1,2,0:T(8,128)} %fusion.11) | data formatting | bytes 22282240 | tf_op jit(solution)/shard_map/kba,kbv->kav/dot_general | solution.py:20
  158.0 10.4 %pad.7 = f32[176,128,128]{2,1,0:T(8,128)} pad(f32[170,128,128]{2,1,0:T(8,128)} %copy.15, f32[]{:T(128)} %constant.31.clone.2), padding=0_6x0_0x0_0 | pad | bytes 22675460
  168.4 18.3 %copy.39 = f32[22,8,128,128]{3,1,2,0:T(8,128)} copy(f32[22,8,128,128]{3,2,1,0:T(8,128)} %bitcast.119) | data formatting | bytes 23068672
  196.4 35.4 %reduce-scatter.7.cloned.1.call-done = f32[256,128]{1,0:T(8,128)} async-done(((f32[2048,128]{1,0:T(8,128)}), f32[256,128]{1,0:T(8,128)}) %reduce-scatter.7.cloned.1.call-update) | async-done | bytes 131088 | tf_op jit(solution)/shard_map/reduce_scatter | solution.py:58
  233.9 144.0 %all-reduce.3.cloned.1.call-done = f32[128,128]{0,1:T(8,128)} async-done(((f32[128,128]{0,1:T(8,128)}), f32[128,128]{0,1:T(8,128)}) %all-reduce.3.cloned.1.call-update) | async-done | bytes 65552 | tf_op jit(solution)/shard_map/psum | solution.py:65
  379.7 11.7 %cholesky.44 = f32[128,128]{1,0:T(8,128)S(1)} custom-call(f32[128,128]{1,0:T(8,128)S(1)} %fusion.27), custom_call_target="Cholesky" | custom-call | tf_op jit(solution)/shard_map/jit(cholesky)/cholesky | solution.py:66
  405.9 20.2 %all_to_all.10 = f32[8,256,128]{2,1,0:T(8,128)S(1)} all-to-all(f32[8,256,128]{2,1,0:T(8,128)S(1)} %stack.11), channel_id=1, replica_groups=mesh['row'=8,'col'=16] {'row'}, dimensions={0} | all-to-all | bytes 2097152 | tf_op jit(solution)/shard_map/all_to_all | solution.py:53
  431.5 23.5 %fusion.14 = f32[170,128,128]{1,2,0:T(8,128)} fusion(f32[170,128,128]{2,1,0:T(8,128)} %gather_fusion.2, f32[1,1,170,128,128]{4,3,2,1,0:T(8,128)} %param.6), kind=kOutput, calls=%fused_computation.14 | convolution fusion | flops 4278190080 | bytes 33423360 | tf_op jit(solution)/shard_map/kab,kbv->kav/dot_general | solution.py:18
  455.0 12.0 %copy.21 = f32[170,128,128]{2,1,0:T(8,128)} copy(f32[170,128,128]{1,2,0:T(8,128)} %fusion.14) | data formatting | bytes 22282240 | tf_op jit(solution)/shard_map/kab,kbv->kav/dot_general | solution.py:18
  467.0 10.3 %pad.8 = f32[176,128,128]{2,1,0:T(8,128)} pad(f32[170,128,128]{2,1,0:T(8,128)} %copy.21, f32[]{:T(128)} %constant.31.clone.2), padding=0_6x0_0x0_0 | pad | bytes 22675460
  477.4 18.3 %copy.40 = f32[22,8,128,128]{3,1,2,0:T(8,128)} copy(f32[22,8,128,128]{3,2,1,0:T(8,128)} %bitcast.120) | data formatting | bytes 23068672
  511.8 23.6 %fusion.17 = f32[170,128,128]{1,2,0:T(8,128)} fusion(f32[170,128,128]{2,1,0:T(8,128)} %gather_fusion.3, f32[1,1,170,128,128]{4,3,2,1,0:T(8,128)} %param.6), kind=kOutput, calls=%fused_computation.15 | convolution fusion | flops 4278190080 | bytes 33423360 | tf_op jit(solution)/shard_map/kba,kbv->kav/dot_general | solution.py:20
  535.4 12.0 %copy.24 = f32[170,128,128]{2,1,0:T(8,128)} copy(f32[170,128,128]{1,2,0:T(8,128)} %fusion.17) | data formatting | bytes 22282240 | tf_op jit(solution)/shard_map/kba,kbv->kav/dot_general | solution.py:20
  547.5 10.4 %pad.9 = f32[176,128,128]{2,1,0:T(8,128)} pad(f32[170,128,128]{2,1,0:T(8,128)} %copy.24, f32[]{:T(128)} %constant.31.clone.2), padding=0_6x0_0x0_0 | pad | bytes 22675460
  557.9 18.4 %copy.41 = f32[22,8,128,128]{3,1,2,0:T(8,128)} copy(f32[22,8,128,128]{3,2,1,0:T(8,128)} %bitcast.115) | data formatting | bytes 23068672
  585.7 31.7 %reduce-scatter.11.cloned.1.call-done = f32[256,128]{1,0:T(8,128)} async-done(((f32[2048,128]{1,0:T(8,128)}), f32[256,128]{1,0:T(8,128)}) %reduce-scatter.11.cloned.1.call-update) | async-done | bytes 131088 | tf_op jit(solution)/shard_map/reduce_scatter | solution.py:58
  619.4 144.8 %all-reduce.5.cloned.1.call-done = f32[128,128]{0,1:T(8,128)} async-done(((f32[128,128]{0,1:T(8,128)}), f32[128,128]{0,1:T(8,128)}) %all-reduce.5.cloned.1.call-update) | async-done | bytes 65552 | tf_op jit(solution)/shard_map/psum | solution.py:65
  766.0 11.7 %cholesky.55 = f32[128,128]{1,0:T(8,128)S(1)} custom-call(f32[128,128]{1,0:T(8,128)S(1)} %fusion.24), custom_call_target="Cholesky" | custom-call | tf_op jit(solution)/shard_map/jit(cholesky)/cholesky | solution.py:66
  (66 shorter events, 112.4 us)
Async XLA Ops:
  6.5 103.8 %all-gather.6.cloned.1.call-start = ((), (), s32[]{:S(2)}) async-start(), calls=%async_computation.13 | async-start | bytes 2228224 | tf_op jit(solution)/shard_map/all_gather | solution.py:55
  9.3 22.8 %all-to-all-start = ((f32[8,256,128]{2,1,0:T(8,128)}), f32[8,256,128]{2,1,0:T(8,128)S(1)}, u32[]{:S(2)}, u32[]{:S(2)}) async-start(f32[8,256,128]{2,1,0:T(8,128)} %stack.10), calls=%async_computation | async-start | bytes 2097152 | tf_op jit(solution)/shard_map/all_to_all | solution.py:53
  16.1 178.9 %reduce-scatter.5.cloned.1.call-start = ((), (), s32[]{:S(2)}) async-start(), calls=%async_computation.6 | async-start | bytes 2228224 | tf_op jit(solution)/shard_map/reduce_scatter | solution.py:57
  110.3 121.6 %reduce-scatter.7.cloned.1.call-start = ((), (), s32[]{:S(2)}) async-start(), calls=%async_computation.7 | async-start | bytes 1179648 | tf_op jit(solution)/shard_map/reduce_scatter | solution.py:58
  194.9 183.0 %all-reduce.3.cloned.1.call-start = ((), (), s32[]{:S(2)}) async-start(), calls=%async_computation.8 | async-start | bytes 131072 | tf_op jit(solution)/shard_map/psum | solution.py:65
  233.8 270.7 %all-gather.4.cloned.1.call-start = ((), (), s32[]{:S(2)}) async-start(), calls=%async_computation.10 | async-start | bytes 2228224 | tf_op jit(solution)/shard_map/all_gather | solution.py:55
  404.5 179.9 %reduce-scatter.9.cloned.1.call-start = ((), (), s32[]{:S(2)}) async-start(), calls=%async_computation.9 | async-start | bytes 2228224 | tf_op jit(solution)/shard_map/reduce_scatter | solution.py:57
  504.5 112.9 %reduce-scatter.11.cloned.1.call-start = ((), (), s32[]{:S(2)}) async-start(), calls=%async_computation.11 | async-start | bytes 1179648 | tf_op jit(solution)/shard_map/reduce_scatter | solution.py:58
  584.3 179.9 %all-reduce.5.cloned.1.call-start = ((), (), s32[]{:S(2)}) async-start(), calls=%async_computation.12 | async-start | bytes 131072 | tf_op jit(solution)/shard_map/psum | solution.py:65
Sparse Core Ops, SparseCore 0:
  9.8 52.9 all-gather.5
  110.4 69.3 reduce-scatter.4
  195.0 36.7 reduce-scatter.6
  236.4 141.4 all-reduce.2
  404.6 46.7 all-gather.3
  504.6 65.4 reduce-scatter.8
  584.4 32.9 reduce-scatter.10
  622.8 141.3 all-reduce.4
